TPU v7x, 256 devices: a whole 4x4x8 slice. The times are simulated.
256 devices in a mesh: span: 16 (over z, x_hi), sp: 8 (over y, x_lo), fsdp: 2 (over core).
Axes of the slice: x: 4 (x_hi: 2, x_lo: 2; x = x_hi * 2 + x_lo), y: 4, z: 8, core: 2. Of those that a mesh axis runs over, the one named last changes fastest.
Arguments:
- query_pre: bfloat16 [2, 16384, 3072], P('fsdp', ('span', 'sp')), may hold values from -12 to 12
- key_pre: bfloat16 [2, 16384, 3072], P('fsdp', ('span', 'sp')), may hold values from -12 to 12
- values: bfloat16 [2, 16384, 3072], P('fsdp', ('span', 'sp')), may hold values from -6 to 6
- cotangent: bfloat16 [2, 16384, 3072], P('fsdp', ('span', 'sp')), may hold values from -6 to 6
- gains: float32 [2, 3072], P(None, 'fsdp'), may hold values from 0.5 to 1.5
- frame_span: int32 [2, 16384], P('fsdp', 'span'), may hold values from 0 to 31, as said below
- denoise_steps: int32 [2, 32], P('fsdp'), may hold values from 1 to 4
Outputs:
- query_grad: bfloat16 [2, 16384, 3072], P('fsdp', ('span', 'sp'))
- key_grad: bfloat16 [2, 16384, 3072], P('fsdp', ('span', 'sp'))
- value_grad: bfloat16 [2, 16384, 3072], P('fsdp', ('span', 'sp'))
- gain_grad: float32 [2, 3072], P(None, 'fsdp')
Inputs may be any that keep to these rules, and one draw needn't show every extreme that they name: `frame_span`: never falls along a video. Group g (tokens g * 1024 to (g + 1) * 1024 - 1) holds frame spans 2 g and 2 g + 1, each from a quarter to three quarters of the group's tokens.
All inputs are finite; a program needn't handle non-finite values.
Results may differ from a plain program's by a relative error of at most 0.0081.
The roundings to bfloat16 on the way count: a program that leaves them out, or rounds other values in their place, can miss the bound.
Values may be sent and summed in bfloat16 or wider, within the bound.
No kernel may reach another device: no remote copies, remote signals or barrier semaphores. Data moves between devices by JAX's collectives and lax.ppermute only.
A program may use at most 128 MiB of HBM per device.

v0:
```python
import jax
import jax.numpy as jnp
from jax import lax
from jax.sharding import PartitionSpec as P

HDIM = 128
EPSILON = 1e-06
NEGATIVE = -1e30


def from_behind(value, axis, steps):
    count = lax.axis_size(axis)
    first, last = (max(0, -steps), min(count, count - steps))
    return lax.ppermute(value, axis, [(source, source + steps) for source in range(first, last)])


def normed(raw_rows, gain_row):
    wide = raw_rows.astype(jnp.float32)
    inverse_rms = lax.rsqrt(jnp.mean(wide * wide, axis=-1, keepdims=True) + EPSILON)
    normal_rows = wide * inverse_rms
    return (normal_rows, inverse_rms, (normal_rows * gain_row).astype(jnp.bfloat16))


def norm_backward(grad_rows, normal_rows, inverse_rms, gain_row):
    upstream = grad_rows.astype(jnp.float32)
    scaled = upstream * gain_row
    inner = jnp.mean(scaled * normal_rows, axis=-1, keepdims=True)
    result = (inverse_rms * (scaled - normal_rows * inner)).astype(jnp.bfloat16)
    return (result, jnp.sum(upstream * normal_rows, axis=0))


def across(left, right):
    return lax.dot_general(
        left, right, (((1,), (1,)), ((), ())), preferred_element_type=jnp.float32
    )


def downward(left, right):
    return lax.dot_general(
        left, right, (((0,), (0,)), ((), ())), preferred_element_type=jnp.float32
    )


def head_grads(
    query_head, grad_head, key_joined, value_joined, joined_mask, step_weight, own_width
):
    score_scale = HDIM ** (-0.5)
    scores = across(query_head, key_joined) * score_scale
    masked = jnp.where(joined_mask, scores, NEGATIVE)
    row_max = jnp.max(masked, axis=1)
    row_total = jnp.sum(jnp.exp(masked - row_max[:, None]), axis=1)
    log_total = row_max + jnp.log(row_total)
    grad_prob = across(grad_head, value_joined)
    probs = jnp.where(joined_mask, jnp.exp(scores - log_total[:, None]), 0.0)
    row_delta = jnp.sum(probs * grad_prob, axis=1)
    factor = step_weight[:, None]
    sgrad = (factor * probs * (grad_prob - row_delta[:, None])).astype(jnp.bfloat16)
    weights = (factor * probs).astype(jnp.bfloat16)
    query_part = jnp.dot(sgrad, key_joined, preferred_element_type=jnp.float32) * score_scale
    key_own_grad = downward(sgrad[:, :own_width], query_head) * score_scale
    value_own_grad = downward(weights[:, :own_width], grad_head)
    return (
        query_part,
        key_own_grad,
        value_own_grad,
        sgrad[:, own_width:],
        weights[:, own_width:],
        log_total,
        row_delta,
    )


def on_device(query_pre, key_pre, values, cotangent, gains, frame_span, denoise_steps):
    gain_full = lax.all_gather(gains, "fsdp", axis=1, tiled=True)
    q_normal, q_inverse, q_ready = normed(query_pre[0], gain_full[0])
    k_normal, k_inverse, k_ready = normed(key_pre[0], gain_full[1])
    heads_query, heads_key, heads_value, heads_grad = (
        lax.all_to_all(q_ready, "sp", split_axis=1, concat_axis=0, tiled=True),
        lax.all_to_all(k_ready, "sp", split_axis=1, concat_axis=0, tiled=True),
        lax.all_to_all(values[0], "sp", split_axis=1, concat_axis=0, tiled=True),
        lax.all_to_all(cotangent[0], "sp", split_axis=1, concat_axis=0, tiled=True),
    )
    head_count = heads_query.shape[1] // HDIM
    own_width = heads_query.shape[0]
    span_ids = frame_span[0]
    step_table = denoise_steps[0].astype(jnp.float32)
    matches = span_ids[:, None] == lax.iota(jnp.int32, step_table.shape[0])[None, :]
    step_weight = jnp.sum(jnp.where(matches, step_table[None, :], 0.0), axis=1)
    group_index = lax.axis_index("span")
    key_prev, value_prev = from_behind((heads_key, heads_value), "span", 1)
    own_mask = span_ids[None, :] <= span_ids[:, None]
    prev_open = group_index > 0
    prev_mask = jnp.broadcast_to(prev_open, own_mask.shape)
    joined_mask = jnp.concatenate([own_mask, prev_mask], axis=1)
    key_joined_all = jnp.concatenate([heads_key, key_prev], axis=0)
    value_joined_all = jnp.concatenate([heads_value, value_prev], axis=0)
    query_parts = []
    key_parts = []
    value_parts = []
    sgrad_list = []
    weight_list = []
    total_list = []
    delta_list = []
    for head_index in range(head_count):
        first = head_index * HDIM
        last = first + HDIM
        outcome = head_grads(
            heads_query[:, first:last],
            heads_grad[:, first:last],
            key_joined_all[:, first:last],
            value_joined_all[:, first:last],
            joined_mask,
            step_weight,
            own_width,
        )
        query_parts.append(outcome[0])
        key_parts.append(outcome[1])
        value_parts.append(outcome[2])
        sgrad_list.append(outcome[3])
        weight_list.append(outcome[4])
        total_list.append(outcome[5])
        delta_list.append(outcome[6])
    query_attn = jnp.concatenate(query_parts, axis=1)
    key_own = jnp.concatenate(key_parts, axis=1)
    value_own = jnp.concatenate(value_parts, axis=1)
    key_terms = []
    value_terms = []
    for head_index in range(head_count):
        first = head_index * HDIM
        last = first + HDIM
        key_terms.append(
            downward(sgrad_list[head_index], heads_query[:, first:last]) * HDIM ** (-0.5)
        )
        value_terms.append(downward(weight_list[head_index], heads_grad[:, first:last]))
    key_back, value_back = from_behind(
        (jnp.concatenate(key_terms, axis=1), jnp.concatenate(value_terms, axis=1)), "span", -1
    )
    key_attn = key_own + key_back
    value_attn = value_own + value_back
    query_tokens, key_tokens, value_tokens = (
        lax.all_to_all(
            query_attn.astype(jnp.bfloat16), "sp", split_axis=0, concat_axis=1, tiled=True
        ),
        lax.all_to_all(
            key_attn.astype(jnp.bfloat16), "sp", split_axis=0, concat_axis=1, tiled=True
        ),
        lax.all_to_all(
            value_attn.astype(jnp.bfloat16), "sp", split_axis=0, concat_axis=1, tiled=True
        ),
    )
    query_back, query_gain = norm_backward(query_tokens, q_normal, q_inverse, gain_full[0])
    key_back_rows, key_gain = norm_backward(key_tokens, k_normal, k_inverse, gain_full[1])
    partial_value = jnp.stack([query_gain, key_gain])
    summed = lax.psum(partial_value, ("span", "sp"))
    gain_grad = lax.psum_scatter(summed, "fsdp", scatter_dimension=1, tiled=True)
    return (query_back[None], key_back_rows[None], value_tokens[None], gain_grad)


def solution(mesh):
    placed = (
        P("fsdp", ("span", "sp"), None),
        P("fsdp", ("span", "sp"), None),
        P("fsdp", ("span", "sp"), None),
        P("fsdp", ("span", "sp"), None),
        P(None, "fsdp"),
        P("fsdp", "span"),
        P("fsdp", None),
    )
    return jax.shard_map(
        on_device,
        mesh=mesh,
        in_specs=placed,
        out_specs=(
            P("fsdp", ("span", "sp"), None),
            P("fsdp", ("span", "sp"), None),
            P("fsdp", ("span", "sp"), None),
            P(None, "fsdp"),
        ),
        check_vma=False,
    )
```

profile of v0, /device:TPU:0, one launch (start us, length us, event | category | flops | bytes accessed | tf_op | source)
XLA Modules:
  0.0 1031.0 jit_solution(12937883028764885410)
XLA Ops:
  9.5 4.2 all-to-all-start.2
  18.8 7.4 all-to-all-done.2
  32.1 9.4 all-to-all-done.1
  41.5 4.3 all-to-all-start.3
  46.3 5.9 collective-permute-start
  53.5 6.6 all-to-all-done.3
  60.1 4.2 all-to-all-start
  72.6 12.8 %all-to-all-done = bf16[128,8,384]{2,0,1:T(8,128)(2,1)} async-done(((bf16[128,8,384]{2,0,1:T(8,128)(2,1)}), bf16[128,8,384]{2,0,1:T(8,128)(2,1)}, u32[]{:S(2)}, u32[]{:S(2)}) %all-to-all-start) | async-done | bytes 786464 | tf_op jit(solution)/shard_map/all_to_all | solution.py:78
  90.4 9.0 fusion.9
  99.4 8.6 exponential_reduce_fusion.2
  108.0 5.4 fusion.68
  113.4 5.4 fusion.61
  118.9 20.2 %fusion.6 = (f32[1024]{0:T(1024)S(1)}, f32[1024]{0:T(1024)S(1)}, f32[1024]{0:T(1024)S(1)}, f32[2048,1024]{0,1:T(8,128)}) fusion(f32[1024]{0:T(1024)S(1)} %log_add_fusion.2, f32[1024,2048]{1,0:T(8,128)} %get-tuple-element.37, pred[1024,1024]{1,0:T(32,128)(4,1)S(1)} %broadcast_compare_fusion, pred[]{:T(512)S(6)} %gt.3, f32[2048,1024]{0,1:T(8,128)} %fusion.68, ...), kind=kOutput, calls=%fused_computation.18 | convolution fusion | flops 569373696 | bytes 53239808 | tf_op jit(solution)/shard_map/dot_general | solution.py:33
  139.1 12.5 %multiply_convert_fusion.2 = (bf16[1024,2048]{1,0:T(8,128)(2,1)S(1)}, bf16[1024,2048]{1,0:T(8,128)(2,1)S(1)}, bf16[1024,2048]{1,0:T(8,128)(2,1)S(1)}, bf16[1024,2048]{1,0:T(8,128)(2,1)S(1)}) fusion(f32[1024]{0:T(1024)S(1)} %select_reduce_fusion, f32[1024]{0:T(1024)S(1)} %log_add_fusion.2, f32[1024,2048]{1,0:T(8,128)} %get-tuple-element.37, ...), kind=kLoop, calls=%fused_computation.26 | loop fusion | flops 33554432 | bytes 51400704 | tf_op jit(solution)/shard_map/convert_element_type | solution.py:58
  168.2 4.9 multiply_convert_fusion.1
  185.2 4.3 all-to-all-start.4
  211.6 21.7 %collective-permute-done.2 = f32[1024,384]{1,0:T(8,128)} collective-permute-done((f32[1024,384]{1,0:T(8,128)}, f32[1024,384]{1,0:T(8,128)}, u32[]{:S(2)}, u32[]{:S(2)}) %collective-permute-start.2) | collective-permute-done | bytes 1572896 | tf_op jit(solution)/shard_map/ppermute | solution.py:14
  235.9 5.6 all-to-all-start.5
  244.2 19.0 %collective-permute-done.3 = f32[1024,384]{0,1:T(8,128)} collective-permute-done((f32[1024,384]{0,1:T(8,128)}, f32[1024,384]{0,1:T(8,128)}, u32[]{:S(2)}, u32[]{:S(2)}) %collective-permute-start.3) | collective-permute-done | bytes 1572896 | tf_op jit(solution)/shard_map/ppermute | solution.py:14
  266.1 10.1 all-to-all-done.5
  276.2 4.2 all-to-all-start.6
  288.2 5.7 all-to-all-done.6
  296.2 37.5 %reduce-scatter.4.cloned.1.call-done = f32[1536,2]{1,0:T(8,128)} async-done(((f32[3072,2]{1,0:T(8,128)}), f32[1536,2]{1,0:T(8,128)}) %reduce-scatter.4.cloned.1.call-update) | async-done | bytes 12304
  335.0 688.9 %psum.8 = f32[2,1536]{1,0:T(2,128)} all-reduce(f32[2,1536]{1,0:T(2,128)S(1)} %copy.105), channel_id=1, replica_groups=mesh['span'=16,'sp'=8,'fsdp'=2] {'span','sp'}, use_global_device_ids=true, to_apply=%region_16.17 | all-reduce | flops 3072 | bytes 24576 | tf_op jit(solution)/shard_map/psum | solution.py:154
  (122 shorter events, 98.4 us)
Async XLA Ops:
  9.5 16.7 %all-to-all-start.2 = ((bf16[128,8,384]{0,2,1:T(8,128)(2,1)}), bf16[128,8,384]{0,2,1:T(8,128)(2,1)}, u32[]{:S(2)}, u32[]{:S(2)}) async-start(bf16[128,8,384]{0,2,1:T(8,128)(2,1)} %bitcast.7), calls=%async_computation.2 | async-start | bytes 1572864 | tf_op jit(solution)/shard_map/all_to_all | solution.py:80
  17.2 28.6 %copy-start.5 = (bf16[1,128,3072]{2,1,0:T(8,128)(2,1)S(1)}, bf16[1,128,3072]{2,1,0:T(8,128)(2,1)}, u32[]{:S(2)}) copy-start(bf16[1,128,3072]{2,1,0:T(8,128)(2,1)} %param.7) | copy-start | bytes 2359300
  26.2 15.2 %all-to-all-start.1 = ((bf16[128,8,384]{2,0,1:T(8,128)(2,1)}), bf16[128,8,384]{2,0,1:T(8,128)(2,1)S(1)}, u32[]{:S(2)}, u32[]{:S(2)}) async-start(bf16[128,8,384]{2,0,1:T(8,128)(2,1)} %multiply_convert_fusion.5), calls=%async_computation.1 | async-start | bytes 1572864 | tf_op jit(solution)/shard_map/all_to_all | solution.py:79
  41.5 22.9 %copy-start.20 = (s32[1,32]{1,0:T(1,128)S(1)}, s32[1,32]{1,0:T(1,128)}, u32[]{:S(2)}) copy-start(s32[1,32]{1,0:T(1,128)} %param.13) | copy-start | bytes 388
  41.5 22.9 %copy-start.19 = (s32[1,1024]{1,0:T(1,128)S(1)}, s32[1,1024]{1,0:T(1,128)}, u32[]{:S(2)}) copy-start(s32[1,1024]{1,0:T(1,128)} %param.12) | copy-start | bytes 12292
  41.5 18.7 %all-to-all-start.3 = ((bf16[128,8,384]{0,2,1:T(8,128)(2,1)}), bf16[128,8,384]{0,2,1:T(8,128)(2,1)}, u32[]{:S(2)}, u32[]{:S(2)}) async-start(bf16[128,8,384]{0,2,1:T(8,128)(2,1)} %bitcast.118), calls=%async_computation.3 | async-start | bytes 1572864 | tf_op jit(solution)/shard_map/all_to_all | solution.py:81
  46.3 39.1 %collective-permute-start = (bf16[1024,384]{1,0:T(8,128)(2,1)S(1)}, bf16[1024,384]{1,0:T(8,128)(2,1)}, u32[]{:S(2)}, u32[]{:S(2)}) collective-permute-start(bf16[1024,384]{1,0:T(8,128)(2,1)S(1)} %bitcast.91), channel_id=1, source_target_pairs={{0,16},{16,32},{32,48},{48,64},{64,80},{80,96},{96,112},{112,128},... | collective-permute-start | bytes 2359304 | tf_op jit(solution)/shard_map/ppermute | solution.py:14
  60.1 25.3 %all-to-all-start = ((bf16[128,8,384]{2,0,1:T(8,128)(2,1)}), bf16[128,8,384]{2,0,1:T(8,128)(2,1)}, u32[]{:S(2)}, u32[]{:S(2)}) async-start(bf16[128,8,384]{2,0,1:T(8,128)(2,1)} %multiply_convert_fusion.6), calls=%async_computation | async-start | bytes 1572864 | tf_op jit(solution)/shard_map/all_to_all | solution.py:78
  69.7 38.3 %collective-permute-start.1 = (bf16[1024,384]{1,0:T(8,128)(2,1)}, bf16[1024,384]{1,0:T(8,128)(2,1)}, u32[]{:S(2)}, u32[]{:S(2)}) collective-permute-start(bf16[1024,384]{1,0:T(8,128)(2,1)} %bitcast.102), channel_id=1, source_target_pairs={{0,16},{16,32},{32,48},{48,64},{64,80},{80,96},{96,112},{112,128},... | collective-permute-start | bytes 2359304 | tf_op jit(solution)/shard_map/ppermute | solution.py:14
  87.7 11.7 %copy-start.1 = (f32[1024,2048]{1,0:T(8,128)}, f32[1024,2048]{1,0:T(8,128)S(1)}, u32[]{:S(2)}) copy-start(f32[1024,2048]{1,0:T(8,128)S(1)} %fusion.75) | copy-start | bytes 25165828
  139.1 12.6 %copy-start.14 = (bf16[8,128,384]{2,1,0:T(8,128)(2,1)S(1)}, bf16[8,128,384]{2,1,0:T(8,128)(2,1)}, u32[]{:S(2)}) copy-start(bf16[8,128,384]{2,1,0:T(8,128)(2,1)} %copy.81) | copy-start | bytes 2359300
  153.3 14.8 %slice-start.2 = ((s8[8388608]{0:T(1024)(128)(4,1)}), s8[4194304]{0:T(1024)(128)(4,1)S(1)}, s32[]{:S(2)}) async-start(s8[8388608]{0:T(1024)(128)(4,1)} %bitcast.89), calls=%async_computation.11 | async-start | bytes 8388608
  155.9 12.2 %slice-start = ((s8[8388608]{0:T(1024)(128)(4,1)}), s8[4194304]{0:T(1024)(128)(4,1)S(1)}, s32[]{:S(2)}) async-start(s8[8388608]{0:T(1024)(128)(4,1)} %bitcast.87), calls=%async_computation.9 | async-start | bytes 8388608
  157.2 10.9 %slice-start.3 = ((s8[8388608]{0:T(1024)(128)(4,1)}), s8[4194304]{0:T(1024)(128)(4,1)S(1)}, s32[]{:S(2)}) async-start(s8[8388608]{0:T(1024)(128)(4,1)} %bitcast.89), calls=%async_computation.12 | async-start | bytes 8388608
  185.2 10.5 %copy-start.18 = (f32[1024,128]{0,1:T(8,128)S(1)}, f32[1024,128]{0,1:T(8,128)}, u32[]{:S(2)}) copy-start(f32[1024,128]{0,1:T(8,128)} %fusion.12) | copy-start | bytes 1572868
  185.2 18.3 %all-to-all-start.4 = ((bf16[8,128,384]{2,1,0:T(8,128)(2,1)}), bf16[8,128,384]{2,1,0:T(8,128)(2,1)}, u32[]{:S(2)}, u32[]{:S(2)}) async-start(bf16[8,128,384]{2,1,0:T(8,128)(2,1)} %pad_maximum_fusion.2), calls=%async_computation.4 | async-start | bytes 1572864 | tf_op jit(solution)/shard_map/all_to_all | solution.py:141
  192.4 41.0 %collective-permute-start.2 = (f32[1024,384]{1,0:T(8,128)}, f32[1024,384]{1,0:T(8,128)}, u32[]{:S(2)}, u32[]{:S(2)}) collective-permute-start(f32[1024,384]{1,0:T(8,128)} %pad_maximum_fusion), channel_id=1, source_target_pairs={{16,0},{32,16},{48,32},{64,48},{80,64},{96,80},{112,96},{128,112},... | collective-permute-start | bytes 4718600 | tf_op jit(solution)/shard_map/ppermute | solution.py:14
  197.0 66.2 %collective-permute-start.3 = (f32[1024,384]{0,1:T(8,128)}, f32[1024,384]{0,1:T(8,128)}, u32[]{:S(2)}, u32[]{:S(2)}) collective-permute-start(f32[1024,384]{0,1:T(8,128)} %pad_maximum_fusion.1), channel_id=1, source_target_pairs={{16,0},{32,16},{48,32},{64,48},{80,64},{96,80},{112,96},{128,112},... | collective-permute-start | bytes 4718600 | tf_op jit(solution)/shard_map/ppermute | solution.py:14
  205.6 27.8 %copy-start.15 = (f32[1024,128]{1,0:T(8,128)S(1)}, f32[1024,128]{1,0:T(8,128)}, u32[]{:S(2)}) copy-start(f32[1024,128]{1,0:T(8,128)} %fusion.38) | copy-start | bytes 1572868
  205.6 27.7 %copy-start.16 = (f32[1024,128]{1,0:T(8,128)S(1)}, f32[1024,128]{1,0:T(8,128)}, u32[]{:S(2)}) copy-start(f32[1024,128]{1,0:T(8,128)} %fusion.44) | copy-start | bytes 1572868
  209.0 32.5 %copy-start.6 = (bf16[1,128,3072]{2,1,0:T(8,128)(2,1)S(1)}, bf16[1,128,3072]{2,1,0:T(8,128)(2,1)}, u32[]{:S(2)}) copy-start(bf16[1,128,3072]{2,1,0:T(8,128)(2,1)} %param.7) | copy-start | bytes 2359300
  235.9 40.3 %all-to-all-start.5 = ((bf16[8,128,384]{2,1,0:T(8,128)(2,1)}), bf16[8,128,384]{2,1,0:T(8,128)(2,1)S(1)}, u32[]{:S(2)}, u32[]{:S(2)}) async-start(bf16[8,128,384]{2,1,0:T(8,128)(2,1)} %bitcast.119), calls=%async_computation.5 | async-start | bytes 1572864 | tf_op jit(solution)/shard_map/all_to_all | solution.py:144
  276.2 17.6 %all-to-all-start.6 = ((bf16[8,128,384]{1,2,0:T(8,128)(2,1)}), bf16[8,128,384]{1,2,0:T(8,128)(2,1)}, u32[]{:S(2)}, u32[]{:S(2)}) async-start(bf16[8,128,384]{1,2,0:T(8,128)(2,1)} %copy_bitcast_fusion), calls=%async_computation.6 | async-start | bytes 1572864 | tf_op jit(solution)/shard_map/all_to_all | solution.py:147
  280.5 53.2 %reduce-scatter.4.cloned.1.call-start = ((), (), s32[]{:S(2)}) async-start(), calls=%async_computation.8 | async-start | bytes 2359296
  (13 other events, 95.5 us)
Sparse Core Ops, SparseCore 0:
  287.0 46.5 reduce-scatter.3
where the time goes:
time: 1040 us; the launch traced here: 1030 us
  blocking collectives  691 us (66%)
  waiting for transfers between devices  130 us (12%)
  matrix products  79.4 us (8%)
  other arithmetic  48.8 us (5%)
  starting transfers between devices  42.3 us (4%)
  local copies, waits for them, and re-layouts  24.5 us (2%)
  between operations  14.8 us (1%)
    psum x1, blocking collectives, on_device(): summed = lax.psum(partial_value, ('span', 'sp'))  689 us
    dot_general x6, matrix products, across(): lax.dot_general(left, right, (((1,), (1,)), ((), ())), preferred_element_...  45 us
    ppermute x4, waiting for transfers between devices, from_behind(): lax.ppermute(value, axis, [(source, source + steps) for source in range(f...  40.7 us
    unnamed x2, waiting for transfers between devices  37.5 us
    dot_general x12, matrix products, downward(): lax.dot_general(left, right, (((0,), (0,)), ((), ())), preferred_element_...  26.4 us
  transfers between devices with their start and end apart: 12, of which 9 were waited for; matrix products, arithmetic and copies ran while one was open for 7% of the time, Pallas kernels for 0%

commit v1 on v0

--- a/solution.py
+++ b/solution.py
@@ -151,7 +151,7 @@
     query_back, query_gain = norm_backward(query_tokens, q_normal, q_inverse, gain_full[0])
     key_back_rows, key_gain = norm_backward(key_tokens, k_normal, k_inverse, gain_full[1])
     partial_value = jnp.stack([query_gain, key_gain])
-    summed = lax.psum(partial_value, ("span", "sp"))
+    summed = lax.psum(lax.psum(partial_value, "span"), "sp")
     gain_grad = lax.psum_scatter(summed, "fsdp", scatter_dimension=1, tiled=True)
     return (query_back[None], key_back_rows[None], value_tokens[None], gain_grad)
 

time: 1040 us -> 460 us (0.44)
  blocking collectives: 691 us -> 113 us
    psum x1 -> x2, blocking collectives: 689 us -> 111 us  [on_device(): summed = lax.psum(lax.psum(partial_value, 'span'), 'sp')]
  transfers between devices with their start and end apart: 12 -> 12, of which waited for: 9 -> 9; matrix products, arithmetic and copies ran while one was open for 7% -> 16% of each run, Pallas kernels for 0% -> 0%
where the time goes in v1:
time: 460 us; the launch traced here: 453 us
  waiting for transfers between devices  130 us (28%)
  blocking collectives  113 us (25%)
  matrix products  79.4 us (17%)
  other arithmetic  48.8 us (11%)
  starting transfers between devices  42.3 us (9%)
  local copies, waits for them, and re-layouts  24.5 us (5%)
  between operations  14.8 us (3%)
    psum x2, blocking collectives, on_device(): summed = lax.psum(lax.psum(partial_value, 'span'), 'sp')  111 us
    dot_general x6, matrix products, across(): lax.dot_general(left, right, (((1,), (1,)), ((), ())), preferred_element_...  45 us
    ppermute x4, waiting for transfers between devices, from_behind(): lax.ppermute(value, axis, [(source, source + steps) for source in range(f...  40.7 us
    unnamed x2, waiting for transfers between devices  37.5 us
    dot_general x12, matrix products, downward(): lax.dot_general(left, right, (((0,), (0,)), ((), ())), preferred_element_...  26.4 us
    convert_element_type x2, other arithmetic, head_grads(): weights = (factor * probs).astype(jnp.bfloat16)  17.4 us
    all_to_all x1, waiting for transfers between devices, on_device(): lax.all_to_all(q_ready, 'sp', split_axis=1, concat_axis=0, tiled=True)  12.8 us
    ppermute x4, starting transfers between devices, from_behind(): lax.ppermute(value, axis, [(source, source + steps) for source in range(f...  11.8 us
  transfers between devices with their start and end apart: 12, of which 9 were waited for; matrix products, arithmetic and copies ran while one was open for 16% of the time, Pallas kernels for 0%

profile of v1, /device:TPU:0, one launch (start us, length us, event | category | flops | bytes accessed | tf_op | source)
XLA Modules:
  0.0 452.7 jit_solution(2285639071626016339)
XLA Ops:
  18.8 7.4 %all-to-all-done.2 = bf16[128,8,384]{0,2,1:T(8,128)(2,1)} async-done(((bf16[128,8,384]{0,2,1:T(8,128)(2,1)}), bf16[128,8,384]{0,2,1:T(8,128)(2,1)}, u32[]{:S(2)}, u32[]{:S(2)}) %all-to-all-start.2) | async-done | bytes 786464 | tf_op jit(solution)/shard_map/all_to_all | solution.py:80
  32.1 9.4 %all-to-all-done.1 = bf16[128,8,384]{2,0,1:T(8,128)(2,1)S(1)} async-done(((bf16[128,8,384]{2,0,1:T(8,128)(2,1)}), bf16[128,8,384]{2,0,1:T(8,128)(2,1)S(1)}, u32[]{:S(2)}, u32[]{:S(2)}) %all-to-all-start.1) | async-done | bytes 786464 | tf_op jit(solution)/shard_map/all_to_all | solution.py:79
  41.5 4.3 all-to-all-start.3
  46.3 5.9 %collective-permute-start = (bf16[1024,384]{1,0:T(8,128)(2,1)S(1)}, bf16[1024,384]{1,0:T(8,128)(2,1)}, u32[]{:S(2)}, u32[]{:S(2)}) collective-permute-start(bf16[1024,384]{1,0:T(8,128)(2,1)S(1)} %bitcast.91), channel_id=1, source_target_pairs={{0,16},{16,32},{32,48},{48,64},{64,80},{80,96},{96,112},{112,128},... | collective-permute-start | bytes 2359304 | tf_op jit(solution)/shard_map/ppermute | solution.py:14
  53.5 6.6 %all-to-all-done.3 = bf16[128,8,384]{0,2,1:T(8,128)(2,1)} async-done(((bf16[128,8,384]{0,2,1:T(8,128)(2,1)}), bf16[128,8,384]{0,2,1:T(8,128)(2,1)}, u32[]{:S(2)}, u32[]{:S(2)}) %all-to-all-start.3) | async-done | bytes 786464 | tf_op jit(solution)/shard_map/all_to_all | solution.py:81
  60.1 4.2 all-to-all-start
  72.6 12.8 %all-to-all-done = bf16[128,8,384]{2,0,1:T(8,128)(2,1)} async-done(((bf16[128,8,384]{2,0,1:T(8,128)(2,1)}), bf16[128,8,384]{2,0,1:T(8,128)(2,1)}, u32[]{:S(2)}, u32[]{:S(2)}) %all-to-all-start) | async-done | bytes 786464 | tf_op jit(solution)/shard_map/all_to_all | solution.py:78
  90.4 9.0 %fusion.9 = (f32[1024]{0:T(1024)S(1)}, f32[1024]{0:T(1024)S(1)}, f32[1024]{0:T(1024)S(1)}, f32[1024,2048]{1,0:T(8,128)}) fusion(pred[1024,1024]{1,0:T(32,128)(4,1)S(1)} %broadcast_compare_fusion, pred[]{:T(512)S(6)} %gt.3, f32[1024,2048]{1,0:T(8,128)S(1)} %fusion.82, f32[1024,2048]{1,0:T(8,128)S(1)} %fusion.75, bf16[1024,384]{1,0:T(8,128)(2,1)S(1)} %bitcast.94, ...), kind=kOutput, calls=%fused_computation.27 | convolution fusion | flops 556790784 | bytes 28061696 | tf_op jit(solution)/shard_map/dot_general | solution.py:33
  99.4 8.6 %exponential_reduce_fusion.2 = (f32[1024]{0:T(1024)S(1)}, f32[1024]{0:T(1024)S(1)}, f32[1024]{0:T(1024)S(1)}) fusion(f32[1024,2048]{1,0:T(8,128)} %get-tuple-element.37, pred[1024,1024]{1,0:T(32,128)(4,1)S(1)} %broadcast_compare_fusion, pred[]{:T(512)S(6)} %gt.3, f32[1024]{0:T(1024)S(1)} %get-tuple-element.22, f32[1024]{0:T(1024)S(1)} %get-tuple-element.24, ...), kind=kLoop, calls=%fused_computation.23 | loop fusion | flops 25162752 | bytes 26238976 | tf_op jit(solution)/shard_map/reduce_sum | solution.py:51
  108.0 5.4 %fusion.68 = f32[2048,1024]{0,1:T(8,128)} fusion(bf16[1024,384]{1,0:T(8,128)(2,1)} %collective-permute-done.1, bf16[1024,384]{1,0:T(8,128)(2,1)S(1)} %bitcast.104, bf16[1024,384]{1,0:T(8,128)(2,1)S(1)} %bitcast.112), kind=kOutput, calls=%fused_computation.105 | convolution fusion | flops 537919488 | bytes 10223616 | tf_op jit(solution)/shard_map/dot_general | solution.py:33
  113.4 5.4 %fusion.61 = f32[2048,1024]{0,1:T(8,128)} fusion(bf16[1024,384]{1,0:T(8,128)(2,1)S(1)} %bitcast.105, bf16[1024,384]{1,0:T(8,128)(2,1)} %collective-permute-done.1, bf16[1024,384]{1,0:T(8,128)(2,1)S(1)} %bitcast.113), kind=kOutput, calls=%fused_computation.99 | convolution fusion | flops 537919488 | bytes 10223616 | tf_op jit(solution)/shard_map/dot_general | solution.py:33
  118.9 20.2 %fusion.6 = (f32[1024]{0:T(1024)S(1)}, f32[1024]{0:T(1024)S(1)}, f32[1024]{0:T(1024)S(1)}, f32[2048,1024]{0,1:T(8,128)}) fusion(f32[1024]{0:T(1024)S(1)} %log_add_fusion.2, f32[1024,2048]{1,0:T(8,128)} %get-tuple-element.37, pred[1024,1024]{1,0:T(32,128)(4,1)S(1)} %broadcast_compare_fusion, pred[]{:T(512)S(6)} %gt.3, f32[2048,1024]{0,1:T(8,128)} %fusion.68, ...), kind=kOutput, calls=%fused_computation.18 | convolution fusion | flops 569373696 | bytes 53239808 | tf_op jit(solution)/shard_map/dot_general | solution.py:33
  139.1 12.5 %multiply_convert_fusion.2 = (bf16[1024,2048]{1,0:T(8,128)(2,1)S(1)}, bf16[1024,2048]{1,0:T(8,128)(2,1)S(1)}, bf16[1024,2048]{1,0:T(8,128)(2,1)S(1)}, bf16[1024,2048]{1,0:T(8,128)(2,1)S(1)}) fusion(f32[1024]{0:T(1024)S(1)} %select_reduce_fusion, f32[1024]{0:T(1024)S(1)} %log_add_fusion.2, f32[1024,2048]{1,0:T(8,128)} %get-tuple-element.37, ...), kind=kLoop, calls=%fused_computation.26 | loop fusion | flops 33554432 | bytes 51400704 | tf_op jit(solution)/shard_map/convert_element_type | solution.py:58
  168.2 4.9 %multiply_convert_fusion.1 = (bf16[1024,2048]{1,0:T(8,128)(2,1)}, bf16[1024,2048]{1,0:T(8,128)(2,1)}) fusion(f32[1024]{0:T(1024)S(1)} %select_reduce_fusion, f32[1024]{0:T(1024)S(1)} %get-tuple-element.40, f32[1024,2048]{1,0:T(8,128)S(1)} %bitcast.88, pred[1024,1024]{1,0:T(32,128)(4,1)S(1)} %broadcast_compare_fusion, pred[]{:T(512)S(6)} %gt.3, ...), kind=kLoop, calls=%fused_computation.25 | loop fusion | flops 16777216 | bytes 26226688 | tf_op jit(solution)/shard_map/convert_element_type | solution.py:58
  185.2 4.3 all-to-all-start.4
  211.6 21.7 %collective-permute-done.2 = f32[1024,384]{1,0:T(8,128)} collective-permute-done((f32[1024,384]{1,0:T(8,128)}, f32[1024,384]{1,0:T(8,128)}, u32[]{:S(2)}, u32[]{:S(2)}) %collective-permute-start.2) | collective-permute-done | bytes 1572896 | tf_op jit(solution)/shard_map/ppermute | solution.py:14
  235.9 5.6 %all-to-all-start.5 = ((bf16[8,128,384]{2,1,0:T(8,128)(2,1)}), bf16[8,128,384]{2,1,0:T(8,128)(2,1)S(1)}, u32[]{:S(2)}, u32[]{:S(2)}) async-start(bf16[8,128,384]{2,1,0:T(8,128)(2,1)} %bitcast.119), calls=%async_computation.5 | async-start | bytes 1572864 | tf_op jit(solution)/shard_map/all_to_all | solution.py:144
  244.2 19.0 %collective-permute-done.3 = f32[1024,384]{0,1:T(8,128)} collective-permute-done((f32[1024,384]{0,1:T(8,128)}, f32[1024,384]{0,1:T(8,128)}, u32[]{:S(2)}, u32[]{:S(2)}) %collective-permute-start.3) | collective-permute-done | bytes 1572896 | tf_op jit(solution)/shard_map/ppermute | solution.py:14
  266.1 10.1 %all-to-all-done.5 = bf16[8,128,384]{2,1,0:T(8,128)(2,1)S(1)} async-done(((bf16[8,128,384]{2,1,0:T(8,128)(2,1)}), bf16[8,128,384]{2,1,0:T(8,128)(2,1)S(1)}, u32[]{:S(2)}, u32[]{:S(2)}) %all-to-all-start.5) | async-done | bytes 786464 | tf_op jit(solution)/shard_map/all_to_all | solution.py:144
  276.2 4.2 all-to-all-start.6
  288.2 5.7 %all-to-all-done.6 = bf16[8,128,384]{1,2,0:T(8,128)(2,1)} async-done(((bf16[8,128,384]{1,2,0:T(8,128)(2,1)}), bf16[8,128,384]{1,2,0:T(8,128)(2,1)}, u32[]{:S(2)}, u32[]{:S(2)}) %all-to-all-start.6) | async-done | bytes 786464 | tf_op jit(solution)/shard_map/all_to_all | solution.py:147
  296.2 37.5 %reduce-scatter.4.cloned.1.call-done = f32[1536,2]{1,0:T(8,128)} async-done(((f32[3072,2]{1,0:T(8,128)}), f32[1536,2]{1,0:T(8,128)}) %reduce-scatter.4.cloned.1.call-update) | async-done | bytes 12304
  335.0 77.2 %psum.17 = f32[2,1536]{1,0:T(2,128)S(1)} all-reduce(f32[2,1536]{1,0:T(2,128)S(1)} %copy.105), channel_id=1, replica_groups=mesh['span'=16,'sp'=8,'fsdp'=2] {'span'}, use_global_device_ids=true, to_apply=%region_16.17 | all-reduce | flops 3072 | bytes 24576 | tf_op jit(solution)/shard_map/psum | solution.py:154
  412.2 33.4 %psum.16 = f32[2,1536]{1,0:T(2,128)} all-reduce(f32[2,1536]{1,0:T(2,128)S(1)} %psum.17), channel_id=1, replica_groups=mesh['span'=16,'sp'=8,'fsdp'=2] {'sp'}, use_global_device_ids=true, to_apply=%region_17.18 | all-reduce | flops 3072 | bytes 24576 | tf_op jit(solution)/shard_map/psum | solution.py:154
  (123 shorter events, 102.6 us)
Async XLA Ops:
  9.5 16.7 %all-to-all-start.2 = ((bf16[128,8,384]{0,2,1:T(8,128)(2,1)}), bf16[128,8,384]{0,2,1:T(8,128)(2,1)}, u32[]{:S(2)}, u32[]{:S(2)}) async-start(bf16[128,8,384]{0,2,1:T(8,128)(2,1)} %bitcast.7), calls=%async_computation.2 | async-start | bytes 1572864 | tf_op jit(solution)/shard_map/all_to_all | solution.py:80
  17.2 28.6 %copy-start.5 = (bf16[1,128,3072]{2,1,0:T(8,128)(2,1)S(1)}, bf16[1,128,3072]{2,1,0:T(8,128)(2,1)}, u32[]{:S(2)}) copy-start(bf16[1,128,3072]{2,1,0:T(8,128)(2,1)} %param.7) | copy-start | bytes 2359300
  26.2 15.2 %all-to-all-start.1 = ((bf16[128,8,384]{2,0,1:T(8,128)(2,1)}), bf16[128,8,384]{2,0,1:T(8,128)(2,1)S(1)}, u32[]{:S(2)}, u32[]{:S(2)}) async-start(bf16[128,8,384]{2,0,1:T(8,128)(2,1)} %multiply_convert_fusion.5), calls=%async_computation.1 | async-start | bytes 1572864 | tf_op jit(solution)/shard_map/all_to_all | solution.py:79
  41.5 22.9 %copy-start.20 = (s32[1,32]{1,0:T(1,128)S(1)}, s32[1,32]{1,0:T(1,128)}, u32[]{:S(2)}) copy-start(s32[1,32]{1,0:T(1,128)} %param.13) | copy-start | bytes 388
  41.5 22.9 %copy-start.19 = (s32[1,1024]{1,0:T(1,128)S(1)}, s32[1,1024]{1,0:T(1,128)}, u32[]{:S(2)}) copy-start(s32[1,1024]{1,0:T(1,128)} %param.12) | copy-start | bytes 12292
  41.5 18.7 %all-to-all-start.3 = ((bf16[128,8,384]{0,2,1:T(8,128)(2,1)}), bf16[128,8,384]{0,2,1:T(8,128)(2,1)}, u32[]{:S(2)}, u32[]{:S(2)}) async-start(bf16[128,8,384]{0,2,1:T(8,128)(2,1)} %bitcast.118), calls=%async_computation.3 | async-start | bytes 1572864 | tf_op jit(solution)/shard_map/all_to_all | solution.py:81
  46.3 39.1 %collective-permute-start = (bf16[1024,384]{1,0:T(8,128)(2,1)S(1)}, bf16[1024,384]{1,0:T(8,128)(2,1)}, u32[]{:S(2)}, u32[]{:S(2)}) collective-permute-start(bf16[1024,384]{1,0:T(8,128)(2,1)S(1)} %bitcast.91), channel_id=1, source_target_pairs={{0,16},{16,32},{32,48},{48,64},{64,80},{80,96},{96,112},{112,128},... | collective-permute-start | bytes 2359304 | tf_op jit(solution)/shard_map/ppermute | solution.py:14
  60.1 25.3 %all-to-all-start = ((bf16[128,8,384]{2,0,1:T(8,128)(2,1)}), bf16[128,8,384]{2,0,1:T(8,128)(2,1)}, u32[]{:S(2)}, u32[]{:S(2)}) async-start(bf16[128,8,384]{2,0,1:T(8,128)(2,1)} %multiply_convert_fusion.6), calls=%async_computation | async-start | bytes 1572864 | tf_op jit(solution)/shard_map/all_to_all | solution.py:78
  69.7 38.3 %collective-permute-start.1 = (bf16[1024,384]{1,0:T(8,128)(2,1)}, bf16[1024,384]{1,0:T(8,128)(2,1)}, u32[]{:S(2)}, u32[]{:S(2)}) collective-permute-start(bf16[1024,384]{1,0:T(8,128)(2,1)} %bitcast.102), channel_id=1, source_target_pairs={{0,16},{16,32},{32,48},{48,64},{64,80},{80,96},{96,112},{112,128},... | collective-permute-start | bytes 2359304 | tf_op jit(solution)/shard_map/ppermute | solution.py:14
  87.7 11.7 %copy-start.1 = (f32[1024,2048]{1,0:T(8,128)}, f32[1024,2048]{1,0:T(8,128)S(1)}, u32[]{:S(2)}) copy-start(f32[1024,2048]{1,0:T(8,128)S(1)} %fusion.75) | copy-start | bytes 25165828
  139.1 12.6 %copy-start.14 = (bf16[8,128,384]{2,1,0:T(8,128)(2,1)S(1)}, bf16[8,128,384]{2,1,0:T(8,128)(2,1)}, u32[]{:S(2)}) copy-start(bf16[8,128,384]{2,1,0:T(8,128)(2,1)} %copy.81) | copy-start | bytes 2359300
  153.3 14.8 %slice-start.2 = ((s8[8388608]{0:T(1024)(128)(4,1)}), s8[4194304]{0:T(1024)(128)(4,1)S(1)}, s32[]{:S(2)}) async-start(s8[8388608]{0:T(1024)(128)(4,1)} %bitcast.89), calls=%async_computation.11 | async-start | bytes 8388608
  155.9 12.2 %slice-start = ((s8[8388608]{0:T(1024)(128)(4,1)}), s8[4194304]{0:T(1024)(128)(4,1)S(1)}, s32[]{:S(2)}) async-start(s8[8388608]{0:T(1024)(128)(4,1)} %bitcast.87), calls=%async_computation.9 | async-start | bytes 8388608
  157.2 10.9 %slice-start.3 = ((s8[8388608]{0:T(1024)(128)(4,1)}), s8[4194304]{0:T(1024)(128)(4,1)S(1)}, s32[]{:S(2)}) async-start(s8[8388608]{0:T(1024)(128)(4,1)} %bitcast.89), calls=%async_computation.12 | async-start | bytes 8388608
  185.2 10.5 %copy-start.18 = (f32[1024,128]{0,1:T(8,128)S(1)}, f32[1024,128]{0,1:T(8,128)}, u32[]{:S(2)}) copy-start(f32[1024,128]{0,1:T(8,128)} %fusion.12) | copy-start | bytes 1572868
  185.2 18.3 %all-to-all-start.4 = ((bf16[8,128,384]{2,1,0:T(8,128)(2,1)}), bf16[8,128,384]{2,1,0:T(8,128)(2,1)}, u32[]{:S(2)}, u32[]{:S(2)}) async-start(bf16[8,128,384]{2,1,0:T(8,128)(2,1)} %pad_maximum_fusion.2), calls=%async_computation.4 | async-start | bytes 1572864 | tf_op jit(solution)/shard_map/all_to_all | solution.py:141
  192.4 41.0 %collective-permute-start.2 = (f32[1024,384]{1,0:T(8,128)}, f32[1024,384]{1,0:T(8,128)}, u32[]{:S(2)}, u32[]{:S(2)}) collective-permute-start(f32[1024,384]{1,0:T(8,128)} %pad_maximum_fusion), channel_id=1, source_target_pairs={{16,0},{32,16},{48,32},{64,48},{80,64},{96,80},{112,96},{128,112},... | collective-permute-start | bytes 4718600 | tf_op jit(solution)/shard_map/ppermute | solution.py:14
  197.0 66.2 %collective-permute-start.3 = (f32[1024,384]{0,1:T(8,128)}, f32[1024,384]{0,1:T(8,128)}, u32[]{:S(2)}, u32[]{:S(2)}) collective-permute-start(f32[1024,384]{0,1:T(8,128)} %pad_maximum_fusion.1), channel_id=1, source_target_pairs={{16,0},{32,16},{48,32},{64,48},{80,64},{96,80},{112,96},{128,112},... | collective-permute-start | bytes 4718600 | tf_op jit(solution)/shard_map/ppermute | solution.py:14
  205.6 27.8 %copy-start.15 = (f32[1024,128]{1,0:T(8,128)S(1)}, f32[1024,128]{1,0:T(8,128)}, u32[]{:S(2)}) copy-start(f32[1024,128]{1,0:T(8,128)} %fusion.38) | copy-start | bytes 1572868
  205.6 27.7 %copy-start.16 = (f32[1024,128]{1,0:T(8,128)S(1)}, f32[1024,128]{1,0:T(8,128)}, u32[]{:S(2)}) copy-start(f32[1024,128]{1,0:T(8,128)} %fusion.44) | copy-start | bytes 1572868
  209.0 32.5 %copy-start.6 = (bf16[1,128,3072]{2,1,0:T(8,128)(2,1)S(1)}, bf16[1,128,3072]{2,1,0:T(8,128)(2,1)}, u32[]{:S(2)}) copy-start(bf16[1,128,3072]{2,1,0:T(8,128)(2,1)} %param.7) | copy-start | bytes 2359300
  235.9 40.3 %all-to-all-start.5 = ((bf16[8,128,384]{2,1,0:T(8,128)(2,1)}), bf16[8,128,384]{2,1,0:T(8,128)(2,1)S(1)}, u32[]{:S(2)}, u32[]{:S(2)}) async-start(bf16[8,128,384]{2,1,0:T(8,128)(2,1)} %bitcast.119), calls=%async_computation.5 | async-start | bytes 1572864 | tf_op jit(solution)/shard_map/all_to_all | solution.py:144
  276.2 17.6 %all-to-all-start.6 = ((bf16[8,128,384]{1,2,0:T(8,128)(2,1)}), bf16[8,128,384]{1,2,0:T(8,128)(2,1)}, u32[]{:S(2)}, u32[]{:S(2)}) async-start(bf16[8,128,384]{1,2,0:T(8,128)(2,1)} %copy_bitcast_fusion), calls=%async_computation.6 | async-start | bytes 1572864 | tf_op jit(solution)/shard_map/all_to_all | solution.py:147
  280.5 53.2 %reduce-scatter.4.cloned.1.call-start = ((), (), s32[]{:S(2)}) async-start(), calls=%async_computation.8 | async-start | bytes 2359296
  (13 other events, 95.5 us)
Sparse Core Ops, SparseCore 0:
  287.0 46.5 reduce-scatter.3
